TPU v7x, 256 devices: a whole 4x4x8 slice. The times are simulated.
256 devices in a mesh: seq: 64 (over y, z, core), ch: 4 (over x).
Axes of the slice: x: 4, y: 4, z: 8, core: 2. Of those that a mesh axis runs over, the one named last changes fastest.
Arguments:
- features: bfloat16 [32768, 1024], P('seq', 'ch'), may hold values from -6 to 6
- w_in: bfloat16 [1024, 3, 1024], P(None, None, 'ch'), may hold values from -0.1875 to 0.1875
- bias_skip: float32 [1024], P('ch'), may hold values from -3 to 3
- filters: float32 [32768, 1024], P('seq', 'ch')
- w_out: bfloat16 [1024, 1024], P(None, 'ch'), may hold values from -0.1875 to 0.1875
- w_emb: bfloat16 [1024, 128], P('ch'), may hold values from -0.1875 to 0.1875
- page_lengths: int32 [512], replicated, may hold values from 1 to 256, 32768 in all
- page_owner: int32 [512], replicated, may hold values from 0 to 63
Outputs:
- index_rows: bfloat16 [32768, 128], P('seq')
Inputs may be any that keep to these rules, and one draw needn't show every extreme that they name: page_lengths sum to 32768, and the longest page has exactly 256 patches.
All inputs are finite; a program needn't handle non-finite values.
Results may differ from a plain program's by a relative error of at most 0.0057.
Values may be sent and summed in bfloat16 or wider, within the bound.
A program may use at most 64 MiB of HBM per device.

v0:
```python
import math
import jax
import jax.numpy as jnp
from jax import lax
from jax.sharding import PartitionSpec as P


def angle_table(first_index, second_index, period):
    product = first_index[:, None] * second_index[None, :] % period
    return product.astype(jnp.float32) * (2.0 * math.pi / period)


def apply_table(table, values):
    return jnp.einsum("ki,qic->qkc", table, values, precision=lax.Precision.HIGHEST)


def long_convolution(signal, filters, seq_count, seq_rank):
    rows_dev, chan_dev = signal.shape
    group_rows = rows_dev // seq_count
    block_count = 2 * seq_count
    fft_length = block_count * rows_dev
    block_index = jnp.arange(block_count, dtype=jnp.int32)
    source_index = jnp.arange(seq_count, dtype=jnp.int32)
    outer_angle = angle_table(block_index, source_index, block_count)
    outer_cos = jnp.cos(outer_angle)
    outer_sin = jnp.sin(outer_angle)
    local_rows = seq_rank * group_rows + jnp.arange(group_rows, dtype=jnp.int32)
    twist_angle = angle_table(block_index, local_rows, fft_length)
    twist_cos = jnp.cos(twist_angle)[:, :, None]
    twist_sin = jnp.sin(twist_angle)[:, :, None]
    inner_index = jnp.arange(rows_dev, dtype=jnp.int32)
    inner_angle = angle_table(inner_index, inner_index, rows_dev)
    inner_cos = jnp.cos(inner_angle)
    inner_sin = jnp.sin(inner_angle)
    signal_blocks, filter_blocks = (
        lax.all_to_all(
            signal.reshape(seq_count, group_rows, chan_dev),
            "seq",
            split_axis=0,
            concat_axis=0,
            tiled=True,
        ),
        lax.all_to_all(
            filters.reshape(seq_count, group_rows, chan_dev),
            "seq",
            split_axis=0,
            concat_axis=0,
            tiled=True,
        ),
    )

    def outer_forward(blocks):
        real_part = jnp.einsum("kj,jic->kic", outer_cos, blocks, precision=lax.Precision.HIGHEST)
        imag_part = -jnp.einsum("kj,jic->kic", outer_sin, blocks, precision=lax.Precision.HIGHEST)
        return jnp.stack(
            [
                real_part * twist_cos + imag_part * twist_sin,
                imag_part * twist_cos - real_part * twist_sin,
            ]
        )

    signal_spec, filter_spec = (
        lax.all_to_all(
            outer_forward(signal_blocks), "seq", split_axis=1, concat_axis=2, tiled=True
        ),
        lax.all_to_all(
            outer_forward(filter_blocks), "seq", split_axis=1, concat_axis=2, tiled=True
        ),
    )

    def inner_forward(spectrum):
        real_in = spectrum[0]
        imag_in = spectrum[1]
        return (
            apply_table(inner_cos, real_in) + apply_table(inner_sin, imag_in),
            apply_table(inner_cos, imag_in) - apply_table(inner_sin, real_in),
        )

    signal_real, signal_imag = inner_forward(signal_spec)
    filter_real, filter_imag = inner_forward(filter_spec)
    product_real = signal_real * filter_real - signal_imag * filter_imag
    product_imag = signal_real * filter_imag + signal_imag * filter_real
    back_real = apply_table(inner_cos, product_real) - apply_table(inner_sin, product_imag)
    back_imag = apply_table(inner_cos, product_imag) + apply_table(inner_sin, product_real)
    returned = lax.all_to_all(
        jnp.stack([back_real, back_imag]), "seq", split_axis=2, concat_axis=1, tiled=True
    )
    turned_real = returned[0] * twist_cos - returned[1] * twist_sin
    turned_imag = returned[0] * twist_sin + returned[1] * twist_cos
    result = (
        jnp.einsum("kj,kic->jic", outer_cos, turned_real, precision=lax.Precision.HIGHEST)
        - jnp.einsum("kj,kic->jic", outer_sin, turned_imag, precision=lax.Precision.HIGHEST)
    ) / fft_length
    back_tokens = lax.all_to_all(result, "seq", split_axis=0, concat_axis=1, tiled=True)
    return back_tokens.reshape(rows_dev, chan_dev)


def source_tokens(page_lengths, page_owner, output_rows):
    page_index = jnp.arange(page_lengths.shape[0], dtype=jnp.int32)
    before = (page_owner[None, :] < page_owner[:, None]) | (
        page_owner[None, :] == page_owner[:, None]
    ) & (page_index[None, :] < page_index[:, None])
    placed_start = jnp.sum(jnp.where(before, page_lengths[None, :], 0), axis=1)
    page_start = jnp.cumsum(page_lengths) - page_lengths
    inside = (output_rows[:, None] >= placed_start[None, :]) & (
        output_rows[:, None] < (placed_start + page_lengths)[None, :]
    )
    offsets = page_start[None, :] + output_rows[:, None] - placed_start[None, :]
    return jnp.sum(jnp.where(inside, offsets, 0), axis=1)


def body(features, w_in, bias_skip, filters, w_out, w_emb, page_lengths, page_owner):
    rows_dev, chan_dev = features.shape
    seq_count = lax.axis_size("seq")
    seq_rank = lax.axis_index("seq")
    flat_in = w_in.reshape(w_in.shape[0], -1)
    weight_rows = flat_in
    projected = jnp.dot(
        lax.all_gather(features, "ch", axis=1, tiled=True),
        weight_rows,
        preferred_element_type=jnp.float32,
    )
    projected = projected.reshape(rows_dev, 3, chan_dev)
    gate_branch = projected[:, 0]
    signal = projected[:, 1] * projected[:, 2]
    convolved = long_convolution(signal, filters, seq_count, seq_rank)
    mixed = ((convolved + bias_skip[None, :] * signal) * gate_branch).astype(jnp.bfloat16)
    weight_rows = w_out
    summed = jnp.dot(
        lax.all_gather(mixed, "ch", axis=1, tiled=True),
        weight_rows,
        preferred_element_type=jnp.float32,
    )
    layer_out = (summed + features.astype(jnp.float32)).astype(jnp.bfloat16)
    output_rows = seq_rank * rows_dev + jnp.arange(rows_dev, dtype=jnp.int32)
    source = source_tokens(page_lengths, page_owner, output_rows)
    embedded = lax.psum(jnp.dot(layer_out, w_emb, preferred_element_type=jnp.float32), "ch").astype(
        jnp.bfloat16
    )
    shard_part = lax.all_gather(embedded, "seq", axis=0, tiled=True)
    count_rows = shard_part.shape[0]
    inside = (source >= 0) & (source < count_rows)
    taken = jnp.take(shard_part, jnp.clip(source, 0, count_rows - 1), axis=0)
    return jnp.where(inside[:, None], taken, jnp.zeros_like(embedded))


def solution(mesh):
    return jax.shard_map(
        body,
        mesh=mesh,
        in_specs=(
            P("seq", "ch"),
            P(None, None, "ch"),
            P("ch"),
            P("seq", "ch"),
            P(None, "ch"),
            P("ch", None),
            P(),
            P(),
        ),
        out_specs=P("seq", None),
        check_vma=False,
    )
```

profile of v0, /device:TPU:1, one launch (start us, length us, event | category | flops | bytes accessed | tf_op | source)
XLA Modules:
  0.0 488.9 jit_solution(5704225290694879429)
XLA Ops:
  7.3 13.2 %all-to-all-start.2 = ((f32[64,8,256]{2,1,0:T(8,128)}), f32[64,8,256]{2,1,0:T(8,128)S(1)}, u32[]{:S(2)}, u32[]{:S(2)}) async-start(f32[64,8,256]{2,1,0:T(8,128)} %bitcast.145), calls=%async_computation.2 | async-start | bytes 1048576 | tf_op jit(solution)/shard_map/all_to_all | solution.py:43
  20.4 1.7 copy.53
  22.1 17.4 %all-gather.4.cloned.1.call-done = bf16[512,1024]{1,0:T(8,128)(2,1)} async-done(((bf16[512,256]{1,0:T(8,128)(2,1)}), bf16[512,1024]{1,0:T(8,128)(2,1)}) %all-gather.4.cloned.1.call-update) | async-done | bytes 1048592 | tf_op jit(solution)/shard_map/all_gather | solution.py:119
  39.6 2.2 fusion
  41.8 1.2 copy-done.2
  43.0 0.9 fusion.89
  43.9 12.0 %all-to-all-start = ((f32[64,8,256]{2,1,0:T(8,128)}), f32[64,8,256]{2,1,0:T(8,128)S(1)}, u32[]{:S(2)}, u32[]{:S(2)}) async-start(f32[64,8,256]{2,1,0:T(8,128)} %fusion.89), calls=%async_computation | async-start | bytes 1048576 | tf_op jit(solution)/shard_map/all_to_all | solution.py:36
  56.0 1.2 convolution_negate_fusion
  57.2 2.2 fusion.84
  59.4 13.8 %all-to-all-done = f32[64,8,256]{2,1,0:T(8,128)S(1)} async-done(((f32[64,8,256]{2,1,0:T(8,128)}), f32[64,8,256]{2,1,0:T(8,128)S(1)}, u32[]{:S(2)}, u32[]{:S(2)}) %all-to-all-start) | async-done | bytes 524320 | tf_op jit(solution)/shard_map/all_to_all | solution.py:36
  73.2 1.2 convolution_negate_fusion.1
  74.4 2.9 add_bitcast_fusion
  77.5 2.5 copy.64
  80.0 6.8 %all-to-all-start.3 = ((f32[2,128,8,256]{3,2,0,1:T(8,128)}), f32[2,128,8,256]{3,2,0,1:T(8,128)S(1)}, u32[]{:S(2)}, u32[]{:S(2)}) async-start(f32[2,128,8,256]{3,2,0,1:T(8,128)} %copy.64), calls=%async_computation.3 | async-start | bytes 4194304 | tf_op jit(solution)/shard_map/all_to_all | solution.py:66
  86.8 1.7 pad_maximum_fusion
  88.5 2.6 copy.56
  91.0 46.9 %all-to-all-done.3 = f32[2,128,8,256]{3,2,0,1:T(8,128)S(1)} async-done(((f32[2,128,8,256]{3,2,0,1:T(8,128)}), f32[2,128,8,256]{3,2,0,1:T(8,128)S(1)}, u32[]{:S(2)}, u32[]{:S(2)}) %all-to-all-start.3) | async-done | bytes 2097184 | tf_op jit(solution)/shard_map/all_to_all | solution.py:66
  138.0 1.3 copy-done.1
  139.3 5.8 %all-to-all-start.1 = ((f32[2,128,8,256]{3,2,0,1:T(8,128)}), f32[2,128,8,256]{3,2,0,1:T(8,128)S(1)}, u32[]{:S(2)}, u32[]{:S(2)}) async-start(f32[2,128,8,256]{3,2,0,1:T(8,128)} %copy.56), calls=%async_computation.1 | async-start | bytes 4194304 | tf_op jit(solution)/shard_map/all_to_all | solution.py:63
  145.1 1.7 copy.65
  147.0 7.2 %fusion.16 = f32[2,256,512]{2,1,0:T(8,128)S(1)} fusion(f32[1,2,64,8,256]{4,3,1,2,0:T(8,128)S(1)} %get-tuple-element.13), kind=kOutput, calls=%fused_computation.34 | convolution fusion | flops 1614282752 | bytes 2097152 | tf_op jit(solution)/shard_map/ki,qic->qkc/dot_general | solution.py:14
  154.2 7.4 %fusion.20 = f32[2,256,512]{2,1,0:T(8,128)S(1)} fusion(f32[1,2,64,8,256]{4,3,1,2,0:T(8,128)S(1)} %get-tuple-element.14), kind=kOutput, calls=%fused_computation.38 | convolution fusion | flops 1614282752 | bytes 2097152 | tf_op jit(solution)/shard_map/ki,qic->qkc/dot_general | solution.py:14
  161.6 8.1 %convolution_subtract_fusion.1 = f32[2,256,512]{2,1,0:T(8,128)} fusion(f32[2,256,512]{2,1,0:T(8,128)S(1)} %fusion.16, f32[1,2,64,8,256]{4,3,1,2,0:T(8,128)S(1)} %get-tuple-element.14), kind=kOutput, calls=%fused_computation.16 | convolution fusion | flops 1614544896 | bytes 3145728 | tf_op jit(solution)/shard_map/ki,qic->qkc/dot_general | solution.py:14
  169.7 8.3 %convolution_add_fusion.1 = f32[2,256,512]{2,1,0:T(8,128)} fusion(f32[2,256,512]{2,1,0:T(8,128)S(1)} %fusion.20, f32[1,2,64,8,256]{4,3,1,2,0:T(8,128)S(1)} %get-tuple-element.13), kind=kOutput, calls=%fused_computation.18 | convolution fusion | flops 1614544896 | bytes 3145728 | tf_op jit(solution)/shard_map/ki,qic->qkc/dot_general | solution.py:14
  178.0 18.3 %all-to-all-done.1 = f32[2,128,8,256]{3,2,0,1:T(8,128)S(1)} async-done(((f32[2,128,8,256]{3,2,0,1:T(8,128)}), f32[2,128,8,256]{3,2,0,1:T(8,128)S(1)}, u32[]{:S(2)}, u32[]{:S(2)}) %all-to-all-start.1) | async-done | bytes 2097184 | tf_op jit(solution)/shard_map/all_to_all | solution.py:63
  196.6 7.2 %fusion.36 = f32[2,256,512]{2,1,0:T(8,128)S(1)} fusion(f32[1,2,64,8,256]{4,3,1,2,0:T(8,128)S(1)} %get-tuple-element.15), kind=kOutput, calls=%fused_computation.54 | convolution fusion | flops 1614282752 | bytes 2097152 | tf_op jit(solution)/shard_map/ki,qic->qkc/dot_general | solution.py:14
  203.8 7.6 %fusion.28 = f32[2,256,512]{2,1,0:T(8,128)S(1)} fusion(f32[1,2,64,8,256]{4,3,1,2,0:T(8,128)S(1)} %get-tuple-element.16), kind=kOutput, calls=%fused_computation.46 | convolution fusion | flops 1614282752 | bytes 2097152 | tf_op jit(solution)/shard_map/ki,qic->qkc/dot_general | solution.py:14
  211.4 7.2 %convolution_add_fusion.2 = f32[2,256,512]{2,1,0:T(8,128)S(1)} fusion(f32[2,256,512]{2,1,0:T(8,128)S(1)} %fusion.36, f32[1,2,64,8,256]{4,3,1,2,0:T(8,128)S(1)} %get-tuple-element.16), kind=kOutput, calls=%fused_computation.19 | convolution fusion | flops 1614544896 | bytes 3145728 | tf_op jit(solution)/shard_map/ki,qic->qkc/dot_general | solution.py:14
  218.6 7.6 %multiply_subtract_fusion = (f32[2,256,512]{2,1,0:T(8,128)S(1)}, f32[2,256,512]{2,1,0:T(8,128)S(1)}) fusion(f32[2,256,512]{2,1,0:T(8,128)S(1)} %copy-done.5, f32[2,256,512]{2,1,0:T(8,128)S(1)} %convolution_add_fusion.2, f32[2,256,512]{2,1,0:T(8,128)S(1)} %copy-done.6, f32[2,256,512]{2,1,0:T(8,128)S(1)} %fusion.28, ...), kind=kOutput, calls=%fused_computation.67 | convolution fusion | flops 1616117760 | bytes 7340032 | tf_op jit(solution)/shard_map/ki,qic->qkc/dot_general | solution.py:14
  226.2 6.3 %fusion.14 = f32[2,256,512]{2,1,0:T(8,128)S(1)} fusion(f32[2,256,512]{2,1,0:T(8,128)S(1)} %get-tuple-element.5), kind=kOutput, calls=%fused_computation.32 | convolution fusion | flops 1614282752 | bytes 2097152 | tf_op jit(solution)/shard_map/ki,qic->qkc/dot_general | solution.py:14
  232.6 6.5 %fusion.10 = f32[2,256,512]{2,1,0:T(8,128)S(1)} fusion(f32[2,256,512]{2,1,0:T(8,128)S(1)} %get-tuple-element.6), kind=kOutput, calls=%fused_computation.28 | convolution fusion | flops 1614282752 | bytes 2097152 | tf_op jit(solution)/shard_map/ki,qic->qkc/dot_general | solution.py:14
  239.1 6.3 %fusion.3 = f32[1,2,512,256]{2,3,1,0:T(8,128)S(1)} fusion(f32[2,256,512]{2,1,0:T(8,128)S(1)} %fusion.14, f32[2,256,512]{2,1,0:T(8,128)S(1)} %get-tuple-element.6), kind=kOutput, calls=%fused_computation.15 | convolution fusion | flops 1614544896 | bytes 3145728 | tf_op jit(solution)/shard_map/ki,qic->qkc/dot_general | solution.py:14
  245.5 6.3 %fusion.2 = f32[1,2,512,256]{2,3,1,0:T(8,128)S(1)} fusion(f32[2,256,512]{2,1,0:T(8,128)S(1)} %fusion.10, f32[2,256,512]{2,1,0:T(8,128)S(1)} %get-tuple-element.5), kind=kOutput, calls=%fused_computation.13 | convolution fusion | flops 1614544896 | bytes 3145728 | tf_op jit(solution)/shard_map/ki,qic->qkc/dot_general | solution.py:14
  252.0 2.5 copy.74
  254.5 57.4 %all_to_all.64 = f32[2,2,512,256]{3,1,0,2:T(2,128)S(1)} all-to-all(f32[2,2,512,256]{3,1,0,2:T(2,128)} %copy.74), channel_id=1, replica_groups=mesh['seq'=64,'ch'=4] {'seq'}, dimensions={2} | all-to-all | bytes 4194304 | tf_op jit(solution)/shard_map/all_to_all | solution.py:85
  312.3 1.1 fusion.190
  314.9 3.0 copy.77
  317.9 1.9 squeeze.30
  319.9 1.0 fusion.44
  320.9 1.0 fusion.4
  322.2 23.0 %all_to_all.65 = f32[64,8,256]{2,1,0:T(8,128)S(1)} all-to-all(f32[64,8,256]{2,1,0:T(8,128)S(1)} %copy.78), channel_id=1, replica_groups=mesh['seq'=64,'ch'=4] {'seq'}, dimensions={0} | all-to-all | bytes 1048576 | tf_op jit(solution)/shard_map/all_to_all | solution.py:94
  345.2 0.9 fusion.62
  346.1 23.0 %all-gather.6.cloned.1.call-done = bf16[512,1024]{1,0:T(8,128)(2,1)} async-done(((bf16[512,256]{1,0:T(8,128)(2,1)}), bf16[512,1024]{1,0:T(8,128)(2,1)}) %all-gather.6.cloned.1.call-update) | async-done | bytes 1048592 | tf_op jit(solution)/shard_map/all_gather | solution.py:130
  369.1 1.8 fusion.6
  371.0 15.8 %all-reduce.1 = bf16[512,128]{1,0:T(8,128)(2,1)} all-reduce(f32[512,128]{1,0:T(8,128)S(1)} %fusion.6), channel_id=1, replica_groups=mesh['seq'=64,'ch'=4] {'ch'}, use_global_device_ids=true, to_apply=%region_4.5 | all-reduce | flops 65536 | bytes 393216 | tf_op jit(solution)/shard_map/psum | solution.py:137
  388.2 87.3 %all-gather.8.cloned.1.call-done = bf16[32768,128]{1,0:T(8,128)(2,1)} async-done(((bf16[512,128]{1,0:T(8,128)(2,1)}), bf16[32768,128]{1,0:T(8,128)(2,1)}) %all-gather.8.cloned.1.call-update) | async-done | bytes 8388624 | tf_op jit(solution)/shard_map/all_gather | solution.py:140
  475.5 5.5 %gather_fusion = bf16[512,128]{1,0:T(8,128)(2,1)S(1)} fusion(bf16[32768,128]{1,0:T(8,128)(2,1)} %all-gather.8.cloned.1.call-done, s32[1024]{0:T(1024)S(1)} %pad_clamp_fusion), kind=kCustom, calls=%fused_computation | custom fusion | bytes 264192 | tf_op jit(solution)/shard_map/jit(_take)/gather | solution.py:143
  481.0 0.9 select_select_fusion
  (51 shorter events, 5.5 us)
Async XLA Ops:
  6.5 362.6 %copy-start = (bf16[1024,256]{1,0:T(8,128)(2,1)S(1)}, bf16[1024,256]{1,0:T(8,128)(2,1)}, u32[]{:S(2)}) copy-start(bf16[1024,256]{1,0:T(8,128)(2,1)} %param.12) | copy-start | bytes 1572868
  6.5 33.0 %all-gather.4.cloned.1.call-start = ((), (), s32[]{:S(2)}) async-start(), calls=%async_computation.6 | async-start | bytes 1310720 | tf_op jit(solution)/shard_map/all_gather | solution.py:119
  7.3 36.6 %all-to-all-start.2 = ((f32[64,8,256]{2,1,0:T(8,128)}), f32[64,8,256]{2,1,0:T(8,128)S(1)}, u32[]{:S(2)}, u32[]{:S(2)}) async-start(f32[64,8,256]{2,1,0:T(8,128)} %bitcast.145), calls=%async_computation.2 | async-start | bytes 1048576 | tf_op jit(solution)/shard_map/all_to_all | solution.py:43
  41.8 1.2 copy-start.2
  43.9 29.3 %all-to-all-start = ((f32[64,8,256]{2,1,0:T(8,128)}), f32[64,8,256]{2,1,0:T(8,128)S(1)}, u32[]{:S(2)}, u32[]{:S(2)}) async-start(f32[64,8,256]{2,1,0:T(8,128)} %fusion.89), calls=%async_computation | async-start | bytes 1048576 | tf_op jit(solution)/shard_map/all_to_all | solution.py:36
  73.2 1.2 copy-start.4
  80.0 57.9 %all-to-all-start.3 = ((f32[2,128,8,256]{3,2,0,1:T(8,128)}), f32[2,128,8,256]{3,2,0,1:T(8,128)S(1)}, u32[]{:S(2)}, u32[]{:S(2)}) async-start(f32[2,128,8,256]{3,2,0,1:T(8,128)} %copy.64), calls=%async_computation.3 | async-start | bytes 4194304 | tf_op jit(solution)/shard_map/all_to_all | solution.py:66
  138.0 1.3 copy-start.1
  139.3 57.0 %all-to-all-start.1 = ((f32[2,128,8,256]{3,2,0,1:T(8,128)}), f32[2,128,8,256]{3,2,0,1:T(8,128)S(1)}, u32[]{:S(2)}, u32[]{:S(2)}) async-start(f32[2,128,8,256]{3,2,0,1:T(8,128)} %copy.56), calls=%async_computation.1 | async-start | bytes 4194304 | tf_op jit(solution)/shard_map/all_to_all | solution.py:63
  145.0 224.1 %all-gather.6.cloned.1.call-start = ((), (), s32[]{:S(2)}) async-start(), calls=%async_computation.7 | async-start | bytes 1310720 | tf_op jit(solution)/shard_map/all_gather | solution.py:130
  211.4 7.2 %copy-start.5 = (f32[2,256,512]{2,1,0:T(8,128)S(1)}, f32[2,256,512]{2,1,0:T(8,128)}, u32[]{:S(2)}) copy-start(f32[2,256,512]{2,1,0:T(8,128)} %convolution_subtract_fusion.1) | copy-start | bytes 3145732
  211.4 7.2 %copy-start.6 = (f32[2,256,512]{2,1,0:T(8,128)S(1)}, f32[2,256,512]{2,1,0:T(8,128)}, u32[]{:S(2)}) copy-start(f32[2,256,512]{2,1,0:T(8,128)} %convolution_add_fusion.1) | copy-start | bytes 3145732
  320.9 24.3 %copy-start.3 = (f32[512,3,256]{2,0,1:T(8,128)S(1)}, f32[512,3,256]{2,0,1:T(8,128)}, u32[]{:S(2)}) copy-start(f32[512,3,256]{2,0,1:T(8,128)} %copy-done.2) | copy-start | bytes 4718596
  320.9 24.3 %copy-start.10 = (f32[256]{0:T(256)S(1)}, f32[256]{0:T(256)}, u32[]{:S(2)}) copy-start(f32[256]{0:T(256)} %param.10) | copy-start | bytes 3076
  322.2 46.9 %copy-start.7 = (bf16[512,256]{1,0:T(8,128)(2,1)S(1)}, bf16[512,256]{1,0:T(8,128)(2,1)}, u32[]{:S(2)}) copy-start(bf16[512,256]{1,0:T(8,128)(2,1)} %param.8) | copy-start | bytes 786436
  322.2 46.9 %copy-start.11 = (bf16[256,128]{1,0:T(8,128)(2,1)S(1)}, bf16[256,128]{1,0:T(8,128)(2,1)}, u32[]{:S(2)}) copy-start(bf16[256,128]{1,0:T(8,128)(2,1)} %param.13) | copy-start | bytes 196612
  346.0 40.8 %copy-start.8 = (s32[512]{0:T(512)S(1)}, s32[512]{0:T(512)}, u32[]{:S(2)}) copy-start(s32[512]{0:T(512)} %param.14) | copy-start | bytes 6148
  346.0 41.3 %copy-start.9 = (s32[512]{0:T(512)S(1)}, s32[512]{0:T(512)}, u32[]{:S(2)}) copy-start(s32[512]{0:T(512)} %param.15) | copy-start | bytes 6148
  346.1 129.5 %all-gather.8.cloned.1.call-start = ((), (), s32[]{:S(2)}) async-start(), calls=%async_computation.8 | async-start | bytes 8519680 | tf_op jit(solution)/shard_map/all_gather | solution.py:140
Sparse Core Ops, SparseCore 0:
  9.1 30.3 all-gather.3
  346.2 22.8 all-gather.5
  386.9 88.5 all-gather.7
where the time goes:
time: 498 us; the launch traced here: 489 us
  waiting for transfers between devices  207 us (42%)
  matrix products  99.6 us (20%)
  blocking collectives  96.2 us (19%)
  starting transfers between devices  37.7 us (8%)
  local copies, waits for them, and re-layouts  28.1 us (6%)
  between operations  13.9 us (3%)
  other arithmetic  5.95 us (1%)
    all_gather x1, waiting for transfers between devices, body(): shard_part = lax.all_gather(embedded, 'seq', axis=0, tiled=True)  87.3 us
    dot_general x12, matrix products, apply_table(): jnp.einsum('ki,qic->qkc', table, values, precision=lax.Precision.HIGHEST)  86.1 us
    all_to_all x1, blocking collectives, long_convolution(): lax.all_to_all(jnp.stack([back_real, back_imag]), 'seq', split_axis=2, co...  57.4 us
    all_to_all x1, waiting for transfers between devices, long_convolution(): lax.all_to_all(outer_forward(filter_blocks), 'seq', split_axis=1, concat_...  46.9 us
    all_gather x1, waiting for transfers between devices, body(): lax.all_gather(mixed, 'ch', axis=1, tiled=True)  23 us
    all_to_all x1, blocking collectives, long_convolution(): lax.all_to_all(result, 'seq', split_axis=0, concat_axis=1, tiled=True)  23 us
    all_to_all x1, waiting for transfers between devices, long_convolution(): lax.all_to_all(outer_forward(signal_blocks), 'seq', split_axis=1, concat_...  18.3 us
    all_gather x1, waiting for transfers between devices, body(): lax.all_gather(features, 'ch', axis=1, tiled=True)  17.4 us
  transfers between devices with their start and end apart: 7, of which 6 were waited for; matrix products, arithmetic and copies ran while one was open for 10% of the time, Pallas kernels for 0%

commit v1 on v0

--- a/solution.py
+++ b/solution.py
@@ -134,9 +134,9 @@
     layer_out = (summed + features.astype(jnp.float32)).astype(jnp.bfloat16)
     output_rows = seq_rank * rows_dev + jnp.arange(rows_dev, dtype=jnp.int32)
     source = source_tokens(page_lengths, page_owner, output_rows)
-    embedded = lax.psum(jnp.dot(layer_out, w_emb, preferred_element_type=jnp.float32), "ch").astype(
-        jnp.bfloat16
-    )
+    embedded = jnp.sum(
+        lax.all_gather(jnp.dot(layer_out, w_emb, preferred_element_type=jnp.float32), "ch"), axis=0
+    ).astype(jnp.bfloat16)
     shard_part = lax.all_gather(embedded, "seq", axis=0, tiled=True)
     count_rows = shard_part.shape[0]
     inside = (source >= 0) & (source < count_rows)

time: 498 us -> 510 us (1.024)
  waiting for transfers between devices: 207 us -> 233 us
  blocking collectives: 96.2 us -> 80.3 us
    all_gather x0 -> x1, waiting for transfers between devices: none -> 27.2 us  [body(): lax.all_gather(jnp.dot(layer_out, w_emb, preferred_element_type=jnp.float...]
    psum x1 -> x0, blocking collectives: 15.8 us -> none  [body(): lax.psum(jnp.dot(layer_out, w_emb, preferred_element_type=jnp.float32), '...]
  transfers between devices with their start and end apart: 7 -> 8, of which waited for: 6 -> 7; matrix products, arithmetic and copies ran while one was open for 10% -> 9% of each run, Pallas kernels for 0% -> 0%
where the time goes in v1:
time: 510 us; the launch traced here: 501 us
  waiting for transfers between devices  233 us (46%)
  matrix products  100 us (20%)
  blocking collectives  80.3 us (16%)
  starting transfers between devices  37.8 us (7%)
  local copies, waits for them, and re-layouts  28.1 us (6%)
  between operations  13.9 us (3%)
  other arithmetic  7.88 us (2%)
    dot_general x12, matrix products, apply_table(): jnp.einsum('ki,qic->qkc', table, values, precision=lax.Precision.HIGHEST)  86.1 us
    all_gather x1, waiting for transfers between devices, body(): shard_part = lax.all_gather(embedded, 'seq', axis=0, tiled=True)  85.1 us
    all_to_all x1, blocking collectives, long_convolution(): lax.all_to_all(jnp.stack([back_real, back_imag]), 'seq', split_axis=2, co...  57.4 us
    all_to_all x1, waiting for transfers between devices, long_convolution(): lax.all_to_all(outer_forward(filter_blocks), 'seq', split_axis=1, concat_...  46.9 us
    all_gather x1, waiting for transfers between devices, body(): lax.all_gather(jnp.dot(layer_out, w_emb, preferred_element_type=jnp.float...  27.2 us
    all_gather x1, waiting for transfers between devices, body(): lax.all_gather(mixed, 'ch', axis=1, tiled=True)  23 us
    all_to_all x1, blocking collectives, long_convolution(): lax.all_to_all(result, 'seq', split_axis=0, concat_axis=1, tiled=True)  23 us
    all_to_all x1, waiting for transfers between devices, long_convolution(): lax.all_to_all(outer_forward(signal_blocks), 'seq', split_axis=1, concat_...  18.3 us
  transfers between devices with their start and end apart: 8, of which 7 were waited for; matrix products, arithmetic and copies ran while one was open for 9% of the time, Pallas kernels for 0%

profile of v1, /device:TPU:1, one launch (start us, length us, event | category | flops | bytes accessed | tf_op | source)
XLA Modules:
  0.0 500.8 jit_solution(7920398619913220441)
XLA Ops:
  7.3 13.2 %all-to-all-start.2 = ((f32[64,8,256]{2,1,0:T(8,128)}), f32[64,8,256]{2,1,0:T(8,128)S(1)}, u32[]{:S(2)}, u32[]{:S(2)}) async-start(f32[64,8,256]{2,1,0:T(8,128)} %bitcast.147), calls=%async_computation.2 | async-start | bytes 1048576 | tf_op jit(solution)/shard_map/all_to_all | solution.py:43
  20.4 1.7 copy.53
  22.1 17.4 %all-gather.6.cloned.1.call-done = bf16[512,1024]{1,0:T(8,128)(2,1)} async-done(((bf16[512,256]{1,0:T(8,128)(2,1)}), bf16[512,1024]{1,0:T(8,128)(2,1)}) %all-gather.6.cloned.1.call-update) | async-done | bytes 1048592 | tf_op jit(solution)/shard_map/all_gather | solution.py:119
  39.6 2.2 fusion
  41.8 1.2 copy-done.2
  43.0 0.9 fusion.89
  43.9 12.0 %all-to-all-start = ((f32[64,8,256]{2,1,0:T(8,128)}), f32[64,8,256]{2,1,0:T(8,128)S(1)}, u32[]{:S(2)}, u32[]{:S(2)}) async-start(f32[64,8,256]{2,1,0:T(8,128)} %fusion.89), calls=%async_computation | async-start | bytes 1048576 | tf_op jit(solution)/shard_map/all_to_all | solution.py:36
  56.0 1.2 convolution_negate_fusion
  57.2 2.2 fusion.84
  59.4 13.8 %all-to-all-done = f32[64,8,256]{2,1,0:T(8,128)S(1)} async-done(((f32[64,8,256]{2,1,0:T(8,128)}), f32[64,8,256]{2,1,0:T(8,128)S(1)}, u32[]{:S(2)}, u32[]{:S(2)}) %all-to-all-start) | async-done | bytes 524320 | tf_op jit(solution)/shard_map/all_to_all | solution.py:36
  73.2 1.2 convolution_negate_fusion.1
  74.4 2.9 add_bitcast_fusion
  77.5 2.5 copy.64
  80.0 6.7 %all-to-all-start.3 = ((f32[2,128,8,256]{3,2,0,1:T(8,128)}), f32[2,128,8,256]{3,2,0,1:T(8,128)S(1)}, u32[]{:S(2)}, u32[]{:S(2)}) async-start(f32[2,128,8,256]{3,2,0,1:T(8,128)} %copy.64), calls=%async_computation.3 | async-start | bytes 4194304 | tf_op jit(solution)/shard_map/all_to_all | solution.py:66
  86.7 1.7 pad_maximum_fusion
  88.4 2.5 copy.56
  91.0 46.9 %all-to-all-done.3 = f32[2,128,8,256]{3,2,0,1:T(8,128)S(1)} async-done(((f32[2,128,8,256]{3,2,0,1:T(8,128)}), f32[2,128,8,256]{3,2,0,1:T(8,128)S(1)}, u32[]{:S(2)}, u32[]{:S(2)}) %all-to-all-start.3) | async-done | bytes 2097184 | tf_op jit(solution)/shard_map/all_to_all | solution.py:66
  137.9 1.3 copy-done.1
  139.2 5.8 %all-to-all-start.1 = ((f32[2,128,8,256]{3,2,0,1:T(8,128)}), f32[2,128,8,256]{3,2,0,1:T(8,128)S(1)}, u32[]{:S(2)}, u32[]{:S(2)}) async-start(f32[2,128,8,256]{3,2,0,1:T(8,128)} %copy.56), calls=%async_computation.1 | async-start | bytes 4194304 | tf_op jit(solution)/shard_map/all_to_all | solution.py:63
  145.0 1.7 copy.65
  146.9 7.2 %fusion.16 = f32[2,256,512]{2,1,0:T(8,128)S(1)} fusion(f32[1,2,64,8,256]{4,3,1,2,0:T(8,128)S(1)} %get-tuple-element.13), kind=kOutput, calls=%fused_computation.34 | convolution fusion | flops 1614282752 | bytes 2097152 | tf_op jit(solution)/shard_map/ki,qic->qkc/dot_general | solution.py:14
  154.1 7.4 %fusion.20 = f32[2,256,512]{2,1,0:T(8,128)S(1)} fusion(f32[1,2,64,8,256]{4,3,1,2,0:T(8,128)S(1)} %get-tuple-element.14), kind=kOutput, calls=%fused_computation.38 | convolution fusion | flops 1614282752 | bytes 2097152 | tf_op jit(solution)/shard_map/ki,qic->qkc/dot_general | solution.py:14
  161.5 8.1 %convolution_subtract_fusion.1 = f32[2,256,512]{2,1,0:T(8,128)} fusion(f32[2,256,512]{2,1,0:T(8,128)S(1)} %fusion.16, f32[1,2,64,8,256]{4,3,1,2,0:T(8,128)S(1)} %get-tuple-element.14), kind=kOutput, calls=%fused_computation.16 | convolution fusion | flops 1614544896 | bytes 3145728 | tf_op jit(solution)/shard_map/ki,qic->qkc/dot_general | solution.py:14
  169.6 8.3 %convolution_add_fusion.1 = f32[2,256,512]{2,1,0:T(8,128)} fusion(f32[2,256,512]{2,1,0:T(8,128)S(1)} %fusion.20, f32[1,2,64,8,256]{4,3,1,2,0:T(8,128)S(1)} %get-tuple-element.13), kind=kOutput, calls=%fused_computation.18 | convolution fusion | flops 1614544896 | bytes 3145728 | tf_op jit(solution)/shard_map/ki,qic->qkc/dot_general | solution.py:14
  177.9 18.3 %all-to-all-done.1 = f32[2,128,8,256]{3,2,0,1:T(8,128)S(1)} async-done(((f32[2,128,8,256]{3,2,0,1:T(8,128)}), f32[2,128,8,256]{3,2,0,1:T(8,128)S(1)}, u32[]{:S(2)}, u32[]{:S(2)}) %all-to-all-start.1) | async-done | bytes 2097184 | tf_op jit(solution)/shard_map/all_to_all | solution.py:63
  196.5 7.2 %fusion.36 = f32[2,256,512]{2,1,0:T(8,128)S(1)} fusion(f32[1,2,64,8,256]{4,3,1,2,0:T(8,128)S(1)} %get-tuple-element.15), kind=kOutput, calls=%fused_computation.54 | convolution fusion | flops 1614282752 | bytes 2097152 | tf_op jit(solution)/shard_map/ki,qic->qkc/dot_general | solution.py:14
  203.7 7.6 %fusion.28 = f32[2,256,512]{2,1,0:T(8,128)S(1)} fusion(f32[1,2,64,8,256]{4,3,1,2,0:T(8,128)S(1)} %get-tuple-element.16), kind=kOutput, calls=%fused_computation.46 | convolution fusion | flops 1614282752 | bytes 2097152 | tf_op jit(solution)/shard_map/ki,qic->qkc/dot_general | solution.py:14
  211.3 7.2 %convolution_add_fusion.2 = f32[2,256,512]{2,1,0:T(8,128)S(1)} fusion(f32[2,256,512]{2,1,0:T(8,128)S(1)} %fusion.36, f32[1,2,64,8,256]{4,3,1,2,0:T(8,128)S(1)} %get-tuple-element.16), kind=kOutput, calls=%fused_computation.19 | convolution fusion | flops 1614544896 | bytes 3145728 | tf_op jit(solution)/shard_map/ki,qic->qkc/dot_general | solution.py:14
  218.5 7.6 %multiply_subtract_fusion = (f32[2,256,512]{2,1,0:T(8,128)S(1)}, f32[2,256,512]{2,1,0:T(8,128)S(1)}) fusion(f32[2,256,512]{2,1,0:T(8,128)S(1)} %copy-done.5, f32[2,256,512]{2,1,0:T(8,128)S(1)} %convolution_add_fusion.2, f32[2,256,512]{2,1,0:T(8,128)S(1)} %copy-done.6, f32[2,256,512]{2,1,0:T(8,128)S(1)} %fusion.28, ...), kind=kOutput, calls=%fused_computation.67 | convolution fusion | flops 1616117760 | bytes 7340032 | tf_op jit(solution)/shard_map/ki,qic->qkc/dot_general | solution.py:14
  226.1 6.3 %fusion.14 = f32[2,256,512]{2,1,0:T(8,128)S(1)} fusion(f32[2,256,512]{2,1,0:T(8,128)S(1)} %get-tuple-element.5), kind=kOutput, calls=%fused_computation.32 | convolution fusion | flops 1614282752 | bytes 2097152 | tf_op jit(solution)/shard_map/ki,qic->qkc/dot_general | solution.py:14
  232.5 6.5 %fusion.10 = f32[2,256,512]{2,1,0:T(8,128)S(1)} fusion(f32[2,256,512]{2,1,0:T(8,128)S(1)} %get-tuple-element.6), kind=kOutput, calls=%fused_computation.28 | convolution fusion | flops 1614282752 | bytes 2097152 | tf_op jit(solution)/shard_map/ki,qic->qkc/dot_general | solution.py:14
  239.0 6.3 %fusion.3 = f32[1,2,512,256]{2,3,1,0:T(8,128)S(1)} fusion(f32[2,256,512]{2,1,0:T(8,128)S(1)} %fusion.14, f32[2,256,512]{2,1,0:T(8,128)S(1)} %get-tuple-element.6), kind=kOutput, calls=%fused_computation.15 | convolution fusion | flops 1614544896 | bytes 3145728 | tf_op jit(solution)/shard_map/ki,qic->qkc/dot_general | solution.py:14
  245.4 6.3 %fusion.2 = f32[1,2,512,256]{2,3,1,0:T(8,128)S(1)} fusion(f32[2,256,512]{2,1,0:T(8,128)S(1)} %fusion.10, f32[2,256,512]{2,1,0:T(8,128)S(1)} %get-tuple-element.5), kind=kOutput, calls=%fused_computation.13 | convolution fusion | flops 1614544896 | bytes 3145728 | tf_op jit(solution)/shard_map/ki,qic->qkc/dot_general | solution.py:14
  251.9 2.5 copy.74
  254.4 57.4 %all_to_all.64 = f32[2,2,512,256]{3,1,0,2:T(2,128)S(1)} all-to-all(f32[2,2,512,256]{3,1,0,2:T(2,128)} %copy.74), channel_id=1, replica_groups=mesh['seq'=64,'ch'=4] {'seq'}, dimensions={2} | all-to-all | bytes 4194304 | tf_op jit(solution)/shard_map/all_to_all | solution.py:85
  312.2 1.1 fusion.190
  314.8 3.0 copy.77
  317.9 1.9 squeeze.30
  319.8 1.0 fusion.44
  320.8 1.0 fusion.4
  322.1 23.0 %all_to_all.65 = f32[64,8,256]{2,1,0:T(8,128)S(1)} all-to-all(f32[64,8,256]{2,1,0:T(8,128)S(1)} %copy.78), channel_id=1, replica_groups=mesh['seq'=64,'ch'=4] {'seq'}, dimensions={0} | all-to-all | bytes 1048576 | tf_op jit(solution)/shard_map/all_to_all | solution.py:94
  346.0 23.0 %all-gather.8.cloned.1.call-done = bf16[512,1024]{1,0:T(8,128)(2,1)} async-done(((bf16[512,256]{1,0:T(8,128)(2,1)}), bf16[512,1024]{1,0:T(8,128)(2,1)}) %all-gather.8.cloned.1.call-update) | async-done | bytes 1048592 | tf_op jit(solution)/shard_map/all_gather | solution.py:130
  369.0 2.5 fusion.6
  371.6 27.2 %all-gather.12.cloned.1.call-done = f32[2048,128]{1,0:T(8,128)} async-done(((f32[512,128]{1,0:T(8,128)}), f32[2048,128]{1,0:T(8,128)}) %all-gather.12.cloned.1.call-update) | async-done | bytes 1048592 | tf_op jit(solution)/shard_map/all_gather | solution.py:138
  398.9 2.0 reduce_sum.29
  402.3 85.1 %all-gather.10.cloned.1.call-done = bf16[32768,128]{1,0:T(8,128)(2,1)} async-done(((bf16[512,128]{1,0:T(8,128)(2,1)}), bf16[32768,128]{1,0:T(8,128)(2,1)}) %all-gather.10.cloned.1.call-update) | async-done | bytes 8388624 | tf_op jit(solution)/shard_map/all_gather | solution.py:140
  487.4 5.5 %gather_fusion = bf16[512,128]{1,0:T(8,128)(2,1)S(1)} fusion(bf16[32768,128]{1,0:T(8,128)(2,1)} %all-gather.10.cloned.1.call-done, s32[1024]{0:T(1024)S(1)} %pad_clamp_fusion), kind=kCustom, calls=%fused_computation | custom fusion | bytes 264192 | tf_op jit(solution)/shard_map/jit(_take)/gather | solution.py:143
  492.9 0.9 select_select_fusion
  (54 shorter events, 6.4 us)
Async XLA Ops:
  6.5 362.5 %copy-start = (bf16[1024,256]{1,0:T(8,128)(2,1)S(1)}, bf16[1024,256]{1,0:T(8,128)(2,1)}, u32[]{:S(2)}) copy-start(bf16[1024,256]{1,0:T(8,128)(2,1)} %param.12) | copy-start | bytes 1572868
  6.5 33.0 %all-gather.6.cloned.1.call-start = ((), (), s32[]{:S(2)}) async-start(), calls=%async_computation.6 | async-start | bytes 1310720 | tf_op jit(solution)/shard_map/all_gather | solution.py:119
  7.3 36.6 %all-to-all-start.2 = ((f32[64,8,256]{2,1,0:T(8,128)}), f32[64,8,256]{2,1,0:T(8,128)S(1)}, u32[]{:S(2)}, u32[]{:S(2)}) async-start(f32[64,8,256]{2,1,0:T(8,128)} %bitcast.147), calls=%async_computation.2 | async-start | bytes 1048576 | tf_op jit(solution)/shard_map/all_to_all | solution.py:43
  41.8 1.2 copy-start.2
  43.9 29.3 %all-to-all-start = ((f32[64,8,256]{2,1,0:T(8,128)}), f32[64,8,256]{2,1,0:T(8,128)S(1)}, u32[]{:S(2)}, u32[]{:S(2)}) async-start(f32[64,8,256]{2,1,0:T(8,128)} %fusion.89), calls=%async_computation | async-start | bytes 1048576 | tf_op jit(solution)/shard_map/all_to_all | solution.py:36
  73.2 1.2 copy-start.4
  80.0 57.9 %all-to-all-start.3 = ((f32[2,128,8,256]{3,2,0,1:T(8,128)}), f32[2,128,8,256]{3,2,0,1:T(8,128)S(1)}, u32[]{:S(2)}, u32[]{:S(2)}) async-start(f32[2,128,8,256]{3,2,0,1:T(8,128)} %copy.64), calls=%async_computation.3 | async-start | bytes 4194304 | tf_op jit(solution)/shard_map/all_to_all | solution.py:66
  137.9 1.3 copy-start.1
  139.2 57.0 %all-to-all-start.1 = ((f32[2,128,8,256]{3,2,0,1:T(8,128)}), f32[2,128,8,256]{3,2,0,1:T(8,128)S(1)}, u32[]{:S(2)}, u32[]{:S(2)}) async-start(f32[2,128,8,256]{3,2,0,1:T(8,128)} %copy.56), calls=%async_computation.1 | async-start | bytes 4194304 | tf_op jit(solution)/shard_map/all_to_all | solution.py:63
  145.0 224.0 %all-gather.8.cloned.1.call-start = ((), (), s32[]{:S(2)}) async-start(), calls=%async_computation.7 | async-start | bytes 1310720 | tf_op jit(solution)/shard_map/all_gather | solution.py:130
  211.3 7.2 %copy-start.5 = (f32[2,256,512]{2,1,0:T(8,128)S(1)}, f32[2,256,512]{2,1,0:T(8,128)}, u32[]{:S(2)}) copy-start(f32[2,256,512]{2,1,0:T(8,128)} %convolution_subtract_fusion.1) | copy-start | bytes 3145732
  211.3 7.2 %copy-start.6 = (f32[2,256,512]{2,1,0:T(8,128)S(1)}, f32[2,256,512]{2,1,0:T(8,128)}, u32[]{:S(2)}) copy-start(f32[2,256,512]{2,1,0:T(8,128)} %convolution_add_fusion.1) | copy-start | bytes 3145732
  320.8 24.3 %copy-start.3 = (f32[512,3,256]{2,0,1:T(8,128)S(1)}, f32[512,3,256]{2,0,1:T(8,128)}, u32[]{:S(2)}) copy-start(f32[512,3,256]{2,0,1:T(8,128)} %copy-done.2) | copy-start | bytes 4718596
  320.8 24.3 %copy-start.10 = (f32[256]{0:T(256)S(1)}, f32[256]{0:T(256)}, u32[]{:S(2)}) copy-start(f32[256]{0:T(256)} %param.10) | copy-start | bytes 3076
  322.1 46.9 %copy-start.7 = (bf16[512,256]{1,0:T(8,128)(2,1)S(1)}, bf16[512,256]{1,0:T(8,128)(2,1)}, u32[]{:S(2)}) copy-start(bf16[512,256]{1,0:T(8,128)(2,1)} %param.8) | copy-start | bytes 786436
  322.1 46.9 %copy-start.11 = (bf16[256,128]{1,0:T(8,128)(2,1)S(1)}, bf16[256,128]{1,0:T(8,128)(2,1)}, u32[]{:S(2)}) copy-start(bf16[256,128]{1,0:T(8,128)(2,1)} %param.13) | copy-start | bytes 196612
  345.9 54.9 %copy-start.8 = (s32[512]{0:T(512)S(1)}, s32[512]{0:T(512)}, u32[]{:S(2)}) copy-start(s32[512]{0:T(512)} %param.14) | copy-start | bytes 6148
  345.9 55.5 %copy-start.9 = (s32[512]{0:T(512)S(1)}, s32[512]{0:T(512)}, u32[]{:S(2)}) copy-start(s32[512]{0:T(512)} %param.15) | copy-start | bytes 6148
  345.9 52.9 %all-gather.12.cloned.1.call-start = ((), (), s32[]{:S(2)}) async-start(), calls=%async_computation.9 | async-start | bytes 1310720 | tf_op jit(solution)/shard_map/all_gather | solution.py:138
  371.6 115.8 %all-gather.10.cloned.1.call-start = ((), (), s32[]{:S(2)}) async-start(), calls=%async_computation.8 | async-start | bytes 8519680 | tf_op jit(solution)/shard_map/all_gather | solution.py:140
Sparse Core Ops, SparseCore 0:
  9.1 30.3 all-gather.5
  346.1 22.8 all-gather.7
  371.7 27.1 all-gather.11
  401.5 85.8 all-gather.9
